TPU v7x, 32 devices: a whole 2x2x4 slice. The times are simulated.
32 devices in a mesh: ty: 4 (over y, x), tx: 8 (over z, core).
Axes of the slice: x: 2, y: 2, z: 4, core: 2. Of those that a mesh axis runs over, the one named last changes fastest.
Arguments:
- block_sums: float32 [4096, 1, 1024], P(('ty', 'tx')), may hold values from -6 to 6
- block_weights: float32 [4096, 1, 1024], P(('ty', 'tx')), may hold values from 0.1 to 2
- block_tile: int32 [4096, 1], P(('ty', 'tx')), may hold values from 0 to 31; in each aligned block of 128 rows (0 to 127, 128 to 255, ...) at most 8 rows name the same one
- block_row: int32 [4096], P(('ty', 'tx')), may hold values from 0 to 127
- prior_weight: float32 [512, 8192], P('ty', 'tx'), may hold values from 0.1 to 1
Outputs:
- solution_field: float32 [512, 8192], P('ty', 'tx')
- residual: float32 [512, 8192], P('ty', 'tx')
Inputs may be any that keep to these rules, and one draw needn't show every extreme that they name: `block_tile`: among the 128 blocks of one log shard no tile is named more than 8 times, a bound that some block reaches.
All inputs are finite; a program needn't handle non-finite values.
Results may differ from a plain program's by a relative error of at most 0.0003.
Values sent between devices are 32-bit elements; how exact they have to be, the bound alone decides.
A program may use at most 64 MiB of HBM per device.

v0:
```python
import jax
import jax.numpy as jnp
from jax import lax
from jax.sharding import PartitionSpec as P

HALF = 32
ITERS = 2


def padded_2(block, sides, width):
    for axis, dim in sides:
        count = lax.axis_size(axis)
        forward = [(i, i + 1) for i in range(count - 1)]
        backward = [(target, source) for source, target in forward]
        low = lax.ppermute(
            lax.slice_in_dim(block, block.shape[dim] - width, None, axis=dim), axis, forward
        )
        high = lax.ppermute(lax.slice_in_dim(block, 0, width, axis=dim), axis, backward)
        block = jnp.concatenate([low, block, high], axis=dim)
    return block


def band_matrix(size, transpose):
    outer = jnp.arange(size + 2 * HALF)[:, None]
    inner = jnp.arange(size)[None, :]
    offset = (outer - inner - HALF).astype(jnp.float32)
    dist = jnp.abs(jnp.arange(-HALF, HALF + 1).astype(jnp.float32))
    scaled_all = dist / (HALF + 1.0)
    total = jnp.sum((1.0 - scaled_all) ** 4 * (1.0 + 4.0 * scaled_all))
    scaled = jnp.abs(offset) / (HALF + 1.0)
    values = (
        jnp.where(jnp.abs(offset) <= HALF, (1.0 - scaled) ** 4 * (1.0 + 4.0 * scaled), 0.0) / total
    )
    if transpose:
        return values.T
    return values


def paired(residual, image):
    return lax.psum((jnp.sum(residual * residual), jnp.sum(residual * image)), ("ty", "tx"))


def shards(block_sums, block_weights, block_tile, block_row, prior_weight):
    devices = lax.axis_size(("ty", "tx"))
    blocks, band, cols = block_sums.shape
    rows = prior_weight.shape[0]
    slots = 2 * blocks // devices
    target = block_tile[:, 0]
    owners = (target[:, None] == jnp.arange(devices, dtype=jnp.int32)[None, :]).astype(jnp.int32)
    rank = jnp.sum((jnp.cumsum(owners, axis=0) - 1) * owners, axis=1)
    position = target * slots + rank
    send_sums = jnp.zeros((devices * slots, band, cols), jnp.float32).at[position].set(block_sums)
    send_weights = (
        jnp.zeros((devices * slots, band, cols), jnp.float32).at[position].set(block_weights)
    )
    send_rows = jnp.zeros((devices * slots,), jnp.int32).at[position].set(block_row)
    got_sums, got_weights, got_rows = (
        lax.all_to_all(
            send_sums.reshape(devices, slots, band, cols),
            ("ty", "tx"),
            split_axis=0,
            concat_axis=0,
            tiled=True,
        ),
        lax.all_to_all(
            send_weights.reshape(devices, slots, band, cols),
            ("ty", "tx"),
            split_axis=0,
            concat_axis=0,
            tiled=True,
        ),
        lax.all_to_all(
            send_rows.reshape(devices, slots), ("ty", "tx"), split_axis=0, concat_axis=0, tiled=True
        ),
    )
    received = devices * slots
    got_rows = got_rows.reshape(received)
    select = (jnp.arange(rows // band, dtype=jnp.int32)[:, None] == got_rows[None, :]).astype(
        jnp.float32
    )
    cell_sums = jnp.dot(
        select, got_sums.reshape(received, band * cols), precision=lax.Precision.HIGHEST
    )
    cell_weights = jnp.dot(
        select, got_weights.reshape(received, band * cols), precision=lax.Precision.HIGHEST
    )
    root = jnp.sqrt(prior_weight + cell_weights)
    right_side = cell_sums / root
    col_band = band_matrix(cols, False)
    row_band = band_matrix(rows, True)

    def operate(field):
        padded = padded_2(root * field, (("ty", 0), ("tx", 1)), HALF)
        across = jnp.dot(padded, col_band, precision=lax.Precision.HIGHEST)
        smoothed = jnp.dot(row_band, across, precision=lax.Precision.HIGHEST)
        return 0.5 * field + root * smoothed

    solution_field = jnp.zeros_like(right_side)
    residual = right_side
    image = operate(residual)
    norm_now, product = paired(residual, image)
    alpha = norm_now / product
    direction, along = (residual, image)
    for step in range(ITERS):
        solution_field = solution_field + alpha * direction
        residual = residual - alpha * along
        if step + 1 < ITERS:
            image = operate(residual)
            norm_next, product = paired(residual, image)
            ratio = norm_next / norm_now
            alpha = norm_next / (product - ratio * norm_next / alpha)
            direction = residual + ratio * direction
            along = image + ratio * along
            norm_now = norm_next
    return (solution_field, residual)


def solution(mesh):
    in_specs = (
        P(("ty", "tx"), None, None),
        P(("ty", "tx"), None, None),
        P(("ty", "tx"), None),
        P(("ty", "tx")),
        P("ty", "tx"),
    )
    out_specs = (P("ty", "tx"), P("ty", "tx"))
    return jax.shard_map(shards, mesh=mesh, in_specs=in_specs, out_specs=out_specs, check_vma=False)
```

profile of v0, /device:TPU:0, one launch (start us, length us, event | category | flops | bytes accessed | tf_op | source)
XLA Modules:
  0.0 223.0 jit_solution(14197574348381532590)
XLA Ops:
  0.6 0.7 fusion.19
  1.4 0.2 reduce_window_sum.11
  1.5 0.8 select_reduce_fusion
  2.4 0.7 fusion.20
  3.0 1.1 scatter_custom_fusion
  4.2 0.7 all_to_all.12
  4.9 7.3 %all-to-all-start = ((s32[32,1,8]{2,1,0:T(1,128)}), s32[32,1,8]{2,1,0:T(1,128)S(1)}, u32[]{:S(2)}, u32[]{:S(2)}) async-start(s32[32,1,8]{2,1,0:T(1,128)} %bitcast.3), calls=%async_computation | async-start | bytes 32768 | tf_op jit(solution)/shard_map/all_to_all | solution.py:72
  12.2 2.6 %scatter_custom_fusion.2 = f32[256,1024]{1,0:T(8,128)} fusion(s32[128]{0:T(128)S(1)} %fusion.20, f32[128,1,1024]{2,1,0:T(1,128)} %param.6, f32[]{:T(128)} %constant.16.clone.1), kind=kCustom, calls=%fused_computation.19 | custom fusion | bytes 1572868 | tf_op jit(solution)/shard_map/scatter | solution.py:54
  14.8 4.5 %all-to-all-done = s32[32,1,8]{2,1,0:T(1,128)S(1)} async-done(((s32[32,1,8]{2,1,0:T(1,128)}), s32[32,1,8]{2,1,0:T(1,128)S(1)}, u32[]{:S(2)}, u32[]{:S(2)}) %all-to-all-start) | async-done | bytes 1056 | tf_op jit(solution)/shard_map/all_to_all | solution.py:72
  19.3 0.0 copy-start
  19.3 2.8 %all-to-all-start.2 = ((f32[32,8,1,1024]{3,1,2,0:T(8,128)}), f32[32,8,1,1024]{3,1,2,0:T(8,128)S(1)}, u32[]{:S(2)}, u32[]{:S(2)}) async-start(f32[32,8,1,1024]{3,1,2,0:T(8,128)} %bitcast.6), calls=%async_computation.2 | async-start | bytes 2097152 | tf_op jit(solution)/shard_map/all_to_all | solution.py:65
  22.1 0.0 copy-done
  22.1 2.2 scatter_custom_fusion.1
  24.2 25.3 %all-to-all-done.2 = f32[32,8,1,1024]{3,1,2,0:T(8,128)S(1)} async-done(((f32[32,8,1,1024]{3,1,2,0:T(8,128)}), f32[32,8,1,1024]{3,1,2,0:T(8,128)S(1)}, u32[]{:S(2)}, u32[]{:S(2)}) %all-to-all-start.2) | async-done | bytes 1048608 | tf_op jit(solution)/shard_map/all_to_all | solution.py:65
  49.5 0.0 copy-start.1
  49.5 2.8 %all-to-all-start.1 = ((f32[32,8,1,1024]{3,1,2,0:T(8,128)}), f32[32,8,1,1024]{3,1,2,0:T(8,128)S(1)}, u32[]{:S(2)}, u32[]{:S(2)}) async-start(f32[32,8,1,1024]{3,1,2,0:T(8,128)} %bitcast.4), calls=%async_computation.1 | async-start | bytes 2097152 | tf_op jit(solution)/shard_map/all_to_all | solution.py:58
  52.3 0.5 broadcast.93
  52.8 0.7 reduce.3
  53.5 0.1 eq.35
  53.6 0.0 copy-done.1
  53.6 0.6 fusion.5
  54.2 25.5 %all-to-all-done.1 = f32[32,8,1,1024]{3,1,2,0:T(8,128)S(1)} async-done(((f32[32,8,1,1024]{3,1,2,0:T(8,128)}), f32[32,8,1,1024]{3,1,2,0:T(8,128)S(1)}, u32[]{:S(2)}, u32[]{:S(2)}) %all-to-all-start.1) | async-done | bytes 1048608 | tf_op jit(solution)/shard_map/all_to_all | solution.py:58
  79.8 0.5 fusion.52
  80.4 1.5 collective-permute-start
  81.9 1.3 collective-permute-start.1
  83.2 2.2 collective-permute-done
  85.4 5.5 %collective-permute-done.1 = f32[32,1024]{1,0:T(8,128)S(1)} collective-permute-done((f32[32,1024]{1,0:T(8,128)S(1)}, f32[32,1024]{1,0:T(8,128)S(1)}, u32[]{:S(2)}, u32[]{:S(2)}) %collective-permute-start.1) | collective-permute-done | bytes 131104 | tf_op jit(solution)/shard_map/ppermute | solution.py:18
  90.9 0.1 pad_maximum_fusion
  90.9 0.1 fusion.49
  91.0 1.3 collective-permute-start.3
  92.3 3.0 %collective-permute-start.2 = (f32[192,32]{1,0:T(8,128)S(1)}, f32[192,32]{1,0:T(8,128)S(1)}, u32[]{:S(2)}, u32[]{:S(2)}) collective-permute-start(f32[192,32]{1,0:T(8,128)S(1)} %get-tuple-element.15), channel_id=1, source_target_pairs={{0,1},{1,2},{2,3},{3,4},{4,5},{5,6},{6,7},{8,9},{9,10},{10,11},{11... | collective-permute-start | bytes 73736 | tf_op jit(solution)/shard_map/ppermute | solution.py:15
  95.4 0.6 multiply_reduce_fusion.4
  96.0 0.0 collective-permute-done.3
  96.0 0.3 collective-permute-done.2
  96.3 0.5 concatenate.13
  96.7 6.3 %fusion.2 = f32[192,1024]{1,0:T(8,128)S(1)} fusion(f32[192,1088]{1,0:T(8,128)S(1)} %concatenate.13, f32[]{:T(128)} %multiply_reduce_fusion.4), kind=kOutput, calls=%fused_computation.7 | convolution fusion | flops 2582511616 | bytes 1622020 | tf_op jit(solution)/shard_map/dot_general | solution.py:94
  103.1 2.1 multiply_reduce_fusion.2
  105.2 41.9 %all-reduce.1 = (f32[]{:T(128)}, f32[]{:T(128)}) all-reduce(f32[]{:T(128)} %get-tuple-element.5, f32[]{:T(128)} %get-tuple-element.4), channel_id=1, replica_groups=mesh['ty'=4,'tx'=8] {'ty','tx'}, use_global_device_ids=true, to_apply=%region_6.7 | all-reduce | flops 2 | bytes 16 | tf_op jit(solution)/shard_map/psum | solution.py:40
  148.4 0.1 fusion.47
  148.5 4.2 %collective-permute-start.4 = (f32[32,1024]{1,0:T(8,128)S(1)}, f32[32,1024]{1,0:T(8,128)S(1)}, u32[]{:S(2)}, u32[]{:S(2)}) collective-permute-start(f32[32,1024]{1,0:T(8,128)S(1)} %get-tuple-element.18), channel_id=1, source_target_pairs={{0,8},{8,16},{16,24},{1,9},{9,17},{17,25},{2,10},{10,18},{18,26},{... | collective-permute-start | bytes 393224 | tf_op jit(solution)/shard_map/ppermute | solution.py:15
  152.7 1.3 collective-permute-start.5
  154.0 1.2 collective-permute-done.4
  155.2 4.9 %collective-permute-done.5 = f32[32,1024]{1,0:T(8,128)S(1)} collective-permute-done((f32[32,1024]{1,0:T(8,128)S(1)}, f32[32,1024]{1,0:T(8,128)S(1)}, u32[]{:S(2)}, u32[]{:S(2)}) %collective-permute-start.5) | collective-permute-done | bytes 131104 | tf_op jit(solution)/shard_map/ppermute | solution.py:18
  160.1 0.1 pad_maximum_fusion.1
  160.1 0.1 fusion.48
  160.2 1.3 collective-permute-start.7
  161.5 3.0 %collective-permute-start.6 = (f32[192,32]{1,0:T(8,128)S(1)}, f32[192,32]{1,0:T(8,128)S(1)}, u32[]{:S(2)}, u32[]{:S(2)}) collective-permute-start(f32[192,32]{1,0:T(8,128)S(1)} %get-tuple-element.13), channel_id=1, source_target_pairs={{0,1},{1,2},{2,3},{3,4},{4,5},{5,6},{6,7},{8,9},{9,10},{10,11},{11... | collective-permute-start | bytes 73736 | tf_op jit(solution)/shard_map/ppermute | solution.py:15
  164.6 0.0 collective-permute-done.7
  164.6 0.9 collective-permute-done.6
  165.5 1.2 concatenate.15
  166.7 7.5 %fusion.1 = f32[192,1024]{1,0:T(8,128)S(1)} fusion(f32[192,1088]{1,0:T(8,128)} %concatenate.15, f32[]{:T(128)} %multiply_reduce_fusion.4), kind=kOutput, calls=%fused_computation.6 | convolution fusion | flops 2582511616 | bytes 1622020 | tf_op jit(solution)/shard_map/dot_general | solution.py:94
  174.2 2.1 multiply_reduce_fusion
  176.3 41.1 %all-reduce = (f32[]{:T(128)}, f32[]{:T(128)}) all-reduce(f32[]{:T(128)} %get-tuple-element.3, f32[]{:T(128)} %get-tuple-element.2), channel_id=1, replica_groups=mesh['ty'=4,'tx'=8] {'ty','tx'}, use_global_device_ids=true, to_apply=%region_11.12 | all-reduce | flops 2 | bytes 16 | tf_op jit(solution)/shard_map/psum | solution.py:40
  221.9 1.2 multiply_subtract_fusion
  (2 shorter events, 0.0 us)
Async XLA Ops:
  4.9 14.4 %all-to-all-start = ((s32[32,1,8]{2,1,0:T(1,128)}), s32[32,1,8]{2,1,0:T(1,128)S(1)}, u32[]{:S(2)}, u32[]{:S(2)}) async-start(s32[32,1,8]{2,1,0:T(1,128)} %bitcast.3), calls=%async_computation | async-start | bytes 32768 | tf_op jit(solution)/shard_map/all_to_all | solution.py:72
  19.3 2.8 %copy-start = (f32[128,1,1024]{2,1,0:T(1,128)S(1)}, f32[128,1,1024]{2,1,0:T(1,128)}, u32[]{:S(2)}) copy-start(f32[128,1,1024]{2,1,0:T(1,128)} %param.5) | copy-start | bytes 1572868
  19.3 30.3 %all-to-all-start.2 = ((f32[32,8,1,1024]{3,1,2,0:T(8,128)}), f32[32,8,1,1024]{3,1,2,0:T(8,128)S(1)}, u32[]{:S(2)}, u32[]{:S(2)}) async-start(f32[32,8,1,1024]{3,1,2,0:T(8,128)} %bitcast.6), calls=%async_computation.2 | async-start | bytes 2097152 | tf_op jit(solution)/shard_map/all_to_all | solution.py:65
  49.5 4.1 %copy-start.1 = (f32[128,1024]{1,0:T(8,128)S(1)}, f32[128,1024]{1,0:T(8,128)}, u32[]{:S(2)}) copy-start(f32[128,1024]{1,0:T(8,128)} %param.9) | copy-start | bytes 1572868
  49.5 30.3 %all-to-all-start.1 = ((f32[32,8,1,1024]{3,1,2,0:T(8,128)}), f32[32,8,1,1024]{3,1,2,0:T(8,128)S(1)}, u32[]{:S(2)}, u32[]{:S(2)}) async-start(f32[32,8,1,1024]{3,1,2,0:T(8,128)} %bitcast.4), calls=%async_computation.1 | async-start | bytes 2097152 | tf_op jit(solution)/shard_map/all_to_all | solution.py:58
  80.4 5.0 %collective-permute-start = (f32[32,1024]{1,0:T(8,128)S(1)}, f32[32,1024]{1,0:T(8,128)S(1)}, u32[]{:S(2)}, u32[]{:S(2)}) collective-permute-start(f32[32,1024]{1,0:T(8,128)S(1)} %get-tuple-element.20), channel_id=1, source_target_pairs={{0,8},{8,16},{16,24},{1,9},{9,17},{17,25},{2,10},{10,18},{18,26},{... | collective-permute-start | bytes 393224 | tf_op jit(solution)/shard_map/ppermute | solution.py:15
  81.9 9.0 %collective-permute-start.1 = (f32[32,1024]{1,0:T(8,128)S(1)}, f32[32,1024]{1,0:T(8,128)S(1)}, u32[]{:S(2)}, u32[]{:S(2)}) collective-permute-start(f32[32,1024]{1,0:T(8,128)S(1)} %get-tuple-element.21), channel_id=1, source_target_pairs={{8,0},{16,8},{24,16},{9,1},{17,9},{25,17},{10,2},{18,10},{26,18},{... | collective-permute-start | bytes 393224 | tf_op jit(solution)/shard_map/ppermute | solution.py:18
  91.0 5.0 %collective-permute-start.3 = (f32[192,32]{1,0:T(8,128)S(1)}, f32[192,32]{1,0:T(8,128)S(1)}, u32[]{:S(2)}, u32[]{:S(2)}) collective-permute-start(f32[192,32]{1,0:T(8,128)S(1)} %get-tuple-element.14), channel_id=1, source_target_pairs={{1,0},{2,1},{3,2},{4,3},{5,4},{6,5},{7,6},{9,8},{10,9},{11,10},{12... | collective-permute-start | bytes 73736 | tf_op jit(solution)/shard_map/ppermute | solution.py:18
  92.3 4.0 %collective-permute-start.2 = (f32[192,32]{1,0:T(8,128)S(1)}, f32[192,32]{1,0:T(8,128)S(1)}, u32[]{:S(2)}, u32[]{:S(2)}) collective-permute-start(f32[192,32]{1,0:T(8,128)S(1)} %get-tuple-element.15), channel_id=1, source_target_pairs={{0,1},{1,2},{2,3},{3,4},{4,5},{5,6},{6,7},{8,9},{9,10},{10,11},{11... | collective-permute-start | bytes 73736 | tf_op jit(solution)/shard_map/ppermute | solution.py:15
  148.5 6.7 %collective-permute-start.4 = (f32[32,1024]{1,0:T(8,128)S(1)}, f32[32,1024]{1,0:T(8,128)S(1)}, u32[]{:S(2)}, u32[]{:S(2)}) collective-permute-start(f32[32,1024]{1,0:T(8,128)S(1)} %get-tuple-element.18), channel_id=1, source_target_pairs={{0,8},{8,16},{16,24},{1,9},{9,17},{17,25},{2,10},{10,18},{18,26},{... | collective-permute-start | bytes 393224 | tf_op jit(solution)/shard_map/ppermute | solution.py:15
  152.7 7.4 %collective-permute-start.5 = (f32[32,1024]{1,0:T(8,128)S(1)}, f32[32,1024]{1,0:T(8,128)S(1)}, u32[]{:S(2)}, u32[]{:S(2)}) collective-permute-start(f32[32,1024]{1,0:T(8,128)S(1)} %get-tuple-element.19), channel_id=1, source_target_pairs={{8,0},{16,8},{24,16},{9,1},{17,9},{25,17},{10,2},{18,10},{26,18},{... | collective-permute-start | bytes 393224 | tf_op jit(solution)/shard_map/ppermute | solution.py:18
  160.2 4.3 %collective-permute-start.7 = (f32[192,32]{1,0:T(8,128)S(1)}, f32[192,32]{1,0:T(8,128)S(1)}, u32[]{:S(2)}, u32[]{:S(2)}) collective-permute-start(f32[192,32]{1,0:T(8,128)S(1)} %get-tuple-element.12), channel_id=1, source_target_pairs={{1,0},{2,1},{3,2},{4,3},{5,4},{6,5},{7,6},{9,8},{10,9},{11,10},{12... | collective-permute-start | bytes 73736 | tf_op jit(solution)/shard_map/ppermute | solution.py:18
  161.5 4.0 %collective-permute-start.6 = (f32[192,32]{1,0:T(8,128)S(1)}, f32[192,32]{1,0:T(8,128)S(1)}, u32[]{:S(2)}, u32[]{:S(2)}) collective-permute-start(f32[192,32]{1,0:T(8,128)S(1)} %get-tuple-element.13), channel_id=1, source_target_pairs={{0,1},{1,2},{2,3},{3,4},{4,5},{5,6},{6,7},{8,9},{9,10},{10,11},{11... | collective-permute-start | bytes 73736 | tf_op jit(solution)/shard_map/ppermute | solution.py:15
where the time goes:
time: 224 us; the launch traced here: 223 us
  blocking collectives  83 us (37%)
  waiting for transfers between devices  70.3 us (31%)
  starting transfers between devices  29.8 us (13%)
  matrix products  19.2 us (9%)
  local copies, waits for them, and re-layouts  9.11 us (4%)
  between operations  6.59 us (3%)
  other arithmetic  5.09 us (2%)
    psum x2, blocking collectives, paired(): lax.psum((jnp.sum(residual * residual), jnp.sum(residual * image)), ('ty'...  83 us
    all_to_all x1, waiting for transfers between devices, shards(): lax.all_to_all(send_sums.reshape(devices, slots, band, cols), ('ty', 'tx'...  25.5 us
    all_to_all x1, waiting for transfers between devices, shards(): lax.all_to_all(send_weights.reshape(devices, slots, band, cols), ('ty', '...  25.3 us
    dot_general x2, matrix products, operate(): across = jnp.dot(padded, col_band, precision=lax.Precision.HIGHEST)  13.8 us
    ppermute x4, starting transfers between devices, padded_2(): lax.ppermute(lax.slice_in_dim(block, block.shape[dim] - width, None, axis...  11.8 us
    ppermute x4, waiting for transfers between devices, padded_2(): lax.ppermute(lax.slice_in_dim(block, 0, width, axis=dim), axis, backward)  10.4 us
    all_to_all x1, starting transfers between devices, shards(): lax.all_to_all(send_rows.reshape(devices, slots), ('ty', 'tx'), split_axi...  7.33 us
    ppermute x4, starting transfers between devices, padded_2(): lax.ppermute(lax.slice_in_dim(block, 0, width, axis=dim), axis, backward)  5.17 us
  transfers between devices with their start and end apart: 11, of which 9 were waited for; matrix products, arithmetic and copies ran while one was open for 3% of the time, Pallas kernels for 0%

commit v1 on v0

v1 whole, which is shorter than its diff:
```python
import functools

import jax
import jax.numpy as jnp
import numpy as np
from jax import lax
from jax.experimental import pallas as pl
from jax.experimental.pallas import tpu as pltpu
from jax.sharding import PartitionSpec as P

HALF = 32
LANES = 128
MESH = pl.DeviceIdType.MESH


def taps_matrix(offset):
    def weight(distance):
        scaled = np.abs(distance) / (HALF + 1.0)
        value = (1.0 - scaled) ** 4 * (1.0 + 4.0 * scaled)
        return np.where(np.abs(distance) <= HALF, value, 0.0)

    total = np.sum(weight(np.arange(-HALF, HALF + 1).astype(np.float64)))
    return (weight(offset.astype(np.float64)) / total).astype(np.float32)


def halves(values):
    high = values.astype(jnp.bfloat16)
    return high, (values - high.astype(jnp.float32)).astype(jnp.bfloat16)


def kernel_matrices(rows, width):
    row = np.arange(rows)[:, None] - (np.arange(rows + 2 * HALF)[None, :] - HALF)
    col = (np.arange(width + 2 * LANES)[:, None] - LANES) - np.arange(width)[None, :]
    row_high, row_low = halves(jnp.asarray(taps_matrix(row)))
    col_high, col_low = halves(jnp.asarray(taps_matrix(col)))
    return jnp.concatenate([row_high, row_low], axis=0), col_high, col_low


def directions():
    return [(dy, dx) for dy in (-1, 0, 1) for dx in (-1, 0, 1) if (dy, dx) != (0, 0)]


def span(step, size, margin, width, sending):
    if step == 0:
        return pl.ds(margin, size)
    if sending:
        return pl.ds(margin, width) if step < 0 else pl.ds(margin + size - width, width)
    return pl.ds(margin + size, width) if step < 0 else pl.ds(margin - width, width)


def solve_kernel(
    ny,
    nx,
    sums_ref,
    weights_ref,
    prior_ref,
    row_ref,
    col_high_ref,
    col_low_ref,
    field_ref,
    residual_ref,
    pad_a,
    pad_b,
    part,
    parts,
    halo_send,
    halo_recv,
    part_send,
    part_recv,
):
    count = ny * nx
    rows, cols = prior_ref.shape
    width = col_high_ref.shape[1]
    ty, tx = lax.axis_index("ty"), lax.axis_index("tx")
    me = ty * nx + tx

    barrier = pltpu.get_barrier_semaphore()

    for pad in (pad_a, pad_b):
        pad[0:HALF, :] = jnp.zeros((HALF, cols + 2 * LANES), jnp.float32)
        pad[HALF + rows :, :] = jnp.zeros((HALF, cols + 2 * LANES), jnp.float32)
        pad[HALF : HALF + rows, 0:LANES] = jnp.zeros((rows, LANES), jnp.float32)
        pad[HALF : HALF + rows, LANES + cols :] = jnp.zeros((rows, LANES), jnp.float32)

    def greet(step, carry):
        other = lax.rem(me + step, count)
        pl.semaphore_signal(
            barrier, inc=1, device_id=(other // nx, lax.rem(other, nx)), device_id_type=MESH
        )
        return carry

    lax.fori_loop(1, count, greet, 0)

    pad_a[HALF : HALF + rows, LANES : LANES + cols] = sums_ref[...]
    root = jnp.sqrt(prior_ref[...] + weights_ref[...])
    pl.semaphore_wait(barrier, count - 1)

    def exchange(pad, phase):
        copies = []
        for index, (dy, dx) in enumerate(directions()):
            copy = pltpu.make_async_remote_copy(
                src_ref=pad.at[
                    span(dy, rows, HALF, HALF, True), span(dx, cols, LANES, LANES, True)
                ],
                dst_ref=pad.at[
                    span(dy, rows, HALF, HALF, False), span(dx, cols, LANES, LANES, False)
                ],
                send_sem=halo_send.at[phase, index],
                recv_sem=halo_recv.at[phase, index],
                device_id=(
                    lax.rem(ty + dy + ny, ny),
                    lax.rem(tx + dx + nx, nx),
                ),
                device_id_type=MESH,
            )
            goes = (ty + dy >= 0) & (ty + dy < ny) & (tx + dx >= 0) & (tx + dx < nx)
            comes = (ty - dy >= 0) & (ty - dy < ny) & (tx - dx >= 0) & (tx - dx < nx)
            copies.append((copy, goes, comes))
            pl.when(goes)(copy.start)
        for copy, goes, comes in copies:
            pl.when(comes)(copy.wait_recv)
        return copies

    def finish(copies):
        for copy, goes, comes in copies:
            pl.when(goes)(copy.wait_send)

    def dot(left, right):
        return jnp.dot(left, right, preferred_element_type=jnp.float32)

    def smooth(pad):
        high, low = halves(pad[...])
        both = dot(row_ref[...], high)
        down = both[:rows] + both[rows:] + dot(row_ref[0:rows, :], low)
        high, low = halves(down)
        stacked = jnp.concatenate([high, low], axis=0)
        pieces = []
        for left in range(0, cols, width):
            window = slice(left, left + width + 2 * LANES)
            both = dot(stacked[:, window], col_high_ref[...])
            pieces.append(both[:rows] + both[rows:] + dot(high[:, window], col_low_ref[...]))
        return jnp.concatenate(pieces, axis=1)

    def total(values):
        return jnp.sum(values, axis=(0, 1), keepdims=True)

    first = exchange(pad_a, 0)
    r0 = sums_ref[...] / root
    u = root * smooth(pad_a)
    pad_b[HALF : HALF + rows, LANES : LANES + cols] = root * u
    second = exchange(pad_b, 1)
    rr, ru = total(r0 * r0), total(r0 * u)
    own = jnp.where(rr > 0.0, ru / rr, 0.0)
    z = root * smooth(pad_b)
    q = own * r0 - u
    g = own * u - z
    lane = lax.broadcasted_iota(jnp.int32, (1, LANES), 1)
    packed = jnp.zeros((1, LANES), jnp.float32)
    for index, value in enumerate((rr, ru, total(q * q), total(q * g), total(r0 * g))):
        packed = jnp.where(lane == index, value, packed)
    part[...] = packed
    parts[pl.ds(me, 1), 0, :] = packed

    def tell(step, carry):
        other = lax.rem(me + step, count)
        pltpu.make_async_remote_copy(
            src_ref=part,
            dst_ref=parts.at[me],
            send_sem=part_send,
            recv_sem=part_recv,
            device_id=(other // nx, lax.rem(other, nx)),
            device_id_type=MESH,
        ).start()
        return carry

    lax.fori_loop(1, count, tell, 0)
    everyone = parts.at[pl.ds(0, count - 1)]
    pltpu.make_async_copy(everyone, everyone, part_recv).wait()

    table = parts[...].reshape(count, LANES)
    rr_d, ru_d, qq_d, qg_d, rg_d = [table[:, i : i + 1] for i in range(5)]
    rr, ru = total(rr_d), total(ru_d)
    mu = ru / rr
    shift = mu - jnp.where(rr_d > 0.0, ru_d / rr_d, 0.0)
    qq = total(qq_d + shift * shift * rr_d)
    qg = total(qg_d + shift * (rg_d - qq_d) + shift * shift * ru_d)
    alpha0 = rr / (0.5 * rr + ru)
    norm = alpha0 * alpha0 * qq
    beta = norm / rr
    alpha1 = norm / (alpha0 * alpha0 * (0.5 * qq + qg) - beta * norm / alpha0)
    q = mu * r0 - u
    r1 = alpha0 * q
    field_ref[...] = alpha0 * r0 + alpha1 * (r1 + beta * r0)
    along = alpha0 * (0.5 * q + mu * u - z) + beta * (0.5 * r0 + u)
    residual_ref[...] = r1 - alpha1 * along

    finish(first)
    finish(second)
    pltpu.make_async_copy(everyone, everyone, part_send).wait()


def solve(ny, nx, cell_sums, cell_weights, prior_weight):
    rows, cols = prior_weight.shape
    count = ny * nx
    width = 2 * LANES
    matrices = kernel_matrices(rows, width)
    vmem = pl.BlockSpec(memory_space=pltpu.VMEM)
    shape = jax.ShapeDtypeStruct((rows, cols), jnp.float32)
    padded = pltpu.VMEM((rows + 2 * HALF, cols + 2 * LANES), jnp.float32)
    return pl.pallas_call(
        functools.partial(solve_kernel, ny, nx),
        out_shape=(shape, shape),
        in_specs=[vmem] * 6,
        out_specs=(vmem, vmem),
        scratch_shapes=[
            padded,
            padded,
            pltpu.VMEM((1, LANES), jnp.float32),
            pltpu.VMEM((count, 1, LANES), jnp.float32),
            pltpu.SemaphoreType.DMA((2, 8)),
            pltpu.SemaphoreType.DMA((2, 8)),
            pltpu.SemaphoreType.DMA,
            pltpu.SemaphoreType.DMA,
        ],
        compiler_params=pltpu.CompilerParams(
            collective_id=0, has_side_effects=True, vmem_limit_bytes=40 * 2**20
        ),
    )(cell_sums, cell_weights, prior_weight, *matrices)


def shards(block_sums, block_weights, block_tile, block_row, prior_weight):
    ny, nx = lax.axis_size("ty"), lax.axis_size("tx")
    devices = ny * nx
    blocks, band, cols = block_sums.shape
    rows = prior_weight.shape[0]
    slots = 2 * blocks // devices
    target = block_tile[:, 0]
    owners = (target[:, None] == jnp.arange(devices, dtype=jnp.int32)[None, :]).astype(jnp.int32)
    rank = jnp.sum((jnp.cumsum(owners, axis=0) - 1) * owners, axis=1)
    position = target * slots + rank
    send_sums = jnp.zeros((devices * slots, band, cols), jnp.float32).at[position].set(block_sums)
    send_weights = (
        jnp.zeros((devices * slots, band, cols), jnp.float32).at[position].set(block_weights)
    )
    send_rows = jnp.zeros((devices * slots,), jnp.int32).at[position].set(block_row)

    def swap(values):
        return lax.all_to_all(values, ("ty", "tx"), split_axis=0, concat_axis=0, tiled=True)

    got_sums = swap(send_sums.reshape(devices, slots, band, cols))
    got_weights = swap(send_weights.reshape(devices, slots, band, cols))
    got_rows = swap(send_rows.reshape(devices, slots))
    received = devices * slots
    got_rows = got_rows.reshape(received)
    select = (jnp.arange(rows // band, dtype=jnp.int32)[:, None] == got_rows[None, :]).astype(
        jnp.float32
    )
    cell_sums = jnp.dot(
        select, got_sums.reshape(received, band * cols), precision=lax.Precision.HIGHEST
    )
    cell_weights = jnp.dot(
        select, got_weights.reshape(received, band * cols), precision=lax.Precision.HIGHEST
    )
    return solve(ny, nx, cell_sums, cell_weights, prior_weight)


def solution(mesh):
    in_specs = (
        P(("ty", "tx"), None, None),
        P(("ty", "tx"), None, None),
        P(("ty", "tx"), None),
        P(("ty", "tx")),
        P("ty", "tx"),
    )
    out_specs = (P("ty", "tx"), P("ty", "tx"))
    return jax.shard_map(shards, mesh=mesh, in_specs=in_specs, out_specs=out_specs, check_vma=False)
```

time: 224 us -> 109 us (0.49)
  blocking collectives: 83 us -> 0 us
  Pallas kernels: 0 us -> 28.3 us
  matrix products: 19.2 us -> 1.02 us
  starting transfers between devices: 29.8 us -> 12.7 us
  waiting for transfers between devices: 70.3 us -> 55.4 us
  between operations: 6.59 us -> 0.8 us
  other arithmetic: 5.09 us -> 1.12 us
    psum x2 -> x0, blocking collectives: 83 us -> none  [paired(): lax.psum((jnp.sum(residual * residual), jnp.sum(residual * image)), ('ty'...]
    pallas_call x0 -> x1, Pallas kernels: none -> 28.3 us  [solve(): pl.pallas_call(functools.partial(solve_kernel, ny, nx), out_shape=(shape,...]
    dot_general x4 -> x0, matrix products: 18 us -> none  [the longest x2 13.8 us: operate(): across = jnp.dot(padded, col_band, precision=lax.Precision.HIGHEST)]
    ppermute x8 -> x0, starting transfers between devices: 17 us -> none  [the longest x4 11.8 us: padded_2(): lax.ppermute(lax.slice_in_dim(block, block.shape[dim] - width, None, axis...]
    ppermute x8 -> x0, waiting for transfers between devices: 15 us -> none  [the longest x4 10.4 us: padded_2(): lax.ppermute(lax.slice_in_dim(block, 0, width, axis=dim), axis, backward)]
    unnamed x4 -> x14, local copies, waits for them, and re-layouts: 0.01 us -> 2.27 us
  transfers between devices with their start and end apart: 11 -> 3, of which waited for: 9 -> 3; matrix products, arithmetic and copies ran while one was open for 3% -> 6% of each run, Pallas kernels for 0% -> 0%
where the time goes in v1:
time: 109 us
  waiting for transfers between devices  55.4 us (51%)
  Pallas kernels  28.3 us (26%)
  starting transfers between devices  12.7 us (12%)
  local copies, waits for them, and re-layouts  9.46 us (9%)
  other arithmetic  1.12 us (1%)
    all_to_all x3, waiting for transfers between devices, swap(): lax.all_to_all(values, ('ty', 'tx'), split_axis=0, concat_axis=0, tiled=T...  55.4 us
    pallas_call x1, Pallas kernels, solve(): pl.pallas_call(functools.partial(solve_kernel, ny, nx), out_shape=(shape,...  28.3 us
    all_to_all x3, starting transfers between devices, swap(): lax.all_to_all(values, ('ty', 'tx'), split_axis=0, concat_axis=0, tiled=T...  12.7 us
    scatter x2, local copies, waits for them, and re-layouts, shards(): jnp.zeros((devices * slots, band, cols), jnp.float32).at[position]  4.79 us
    unnamed x14, local copies, waits for them, and re-layouts  2.27 us
  transfers between devices with their start and end apart: 3, of which 3 were waited for; matrix products, arithmetic and copies ran while one was open for 6% of the time, Pallas kernels for 0%

profile of v1, /device:TPU:0, one launch (start us, length us, event | category | flops | bytes accessed | tf_op | source)
XLA Modules:
  0.0 108.8 jit_solution(16358278148970577359)
XLA Ops:
  0.6 0.0 copy-start.5
  0.6 0.6 copy-done.5
  1.3 0.1 fusion.14
  1.4 0.2 reduce_window_sum.11
  1.5 0.2 select_reduce_fusion
  1.7 1.1 %scatter_custom_fusion = s32[256]{0:T(256)S(1)} fusion(s32[128]{0:T(128)S(1)} %fusion.15, s32[128]{0:T(128)} %param.10, s32[]{:T(128)} %constant.7.clone.1), kind=kCustom, calls=%fused_computation.24 | custom fusion | bytes 1536 | tf_op jit(solution)/shard_map/scatter | solution.py:245
  2.9 0.7 all_to_all.12
  3.5 7.3 %all-to-all-start = ((s32[32,1,8]{2,1,0:T(1,128)}), s32[32,1,8]{2,1,0:T(1,128)S(1)}, u32[]{:S(2)}, u32[]{:S(2)}) async-start(s32[32,1,8]{2,1,0:T(1,128)} %bitcast.3), calls=%async_computation | async-start | bytes 32768 | tf_op jit(solution)/shard_map/all_to_all | solution.py:248
  10.9 2.7 %scatter_custom_fusion.2 = f32[256,1024]{1,0:T(8,128)} fusion(s32[128]{0:T(128)S(1)} %fusion.15, f32[128,1,1024]{2,1,0:T(1,128)} %param.8, f32[]{:T(128)} %constant.20.clone.1), kind=kCustom, calls=%fused_computation.7 | custom fusion | bytes 1572868 | tf_op jit(solution)/shard_map/scatter | solution.py:243
  13.6 4.4 %all-to-all-done = s32[32,1,8]{2,1,0:T(1,128)S(1)} async-done(((s32[32,1,8]{2,1,0:T(1,128)}), s32[32,1,8]{2,1,0:T(1,128)S(1)}, u32[]{:S(2)}, u32[]{:S(2)}) %all-to-all-start) | async-done | bytes 1056 | tf_op jit(solution)/shard_map/all_to_all | solution.py:248
  18.0 0.0 copy-start.4
  18.0 2.8 %all-to-all-start.2 = ((f32[32,8,1,1024]{3,1,2,0:T(8,128)}), f32[32,8,1,1024]{3,1,2,0:T(8,128)S(1)}, u32[]{:S(2)}, u32[]{:S(2)}) async-start(f32[32,8,1,1024]{3,1,2,0:T(8,128)} %bitcast.6), calls=%async_computation.2 | async-start | bytes 2097152 | tf_op jit(solution)/shard_map/all_to_all | solution.py:248
  20.8 0.0 copy-done.4
  20.8 2.1 %scatter_custom_fusion.1 = f32[256,1024]{1,0:T(8,128)} fusion(s32[128]{0:T(128)S(1)} %fusion.15, f32[128,1,1024]{2,1,0:T(1,128)S(1)} %copy-done.4, f32[]{:T(128)} %constant.20.clone.1), kind=kCustom, calls=%fused_computation.10 | custom fusion | bytes 1572868 | tf_op jit(solution)/shard_map/scatter | solution.py:241
  22.9 25.3 %all-to-all-done.2 = f32[32,8,1,1024]{3,1,2,0:T(8,128)S(1)} async-done(((f32[32,8,1,1024]{3,1,2,0:T(8,128)}), f32[32,8,1,1024]{3,1,2,0:T(8,128)S(1)}, u32[]{:S(2)}, u32[]{:S(2)}) %all-to-all-start.2) | async-done | bytes 1048608 | tf_op jit(solution)/shard_map/all_to_all | solution.py:248
  48.2 2.6 %all-to-all-start.1 = ((f32[32,8,1,1024]{3,1,2,0:T(8,128)}), f32[32,8,1,1024]{3,1,2,0:T(8,128)S(1)}, u32[]{:S(2)}, u32[]{:S(2)}) async-start(f32[32,8,1,1024]{3,1,2,0:T(8,128)} %bitcast.4), calls=%async_computation.1 | async-start | bytes 2097152 | tf_op jit(solution)/shard_map/all_to_all | solution.py:248
  50.9 0.5 broadcast.37
  51.4 0.7 reduce.3
  52.1 0.1 eq.35
  52.2 0.5 fusion.weights_ref
  52.7 0.0 copy-start
  52.7 0.0 copy-start.1
  52.7 0.0 copy-start.2
  52.7 0.0 copy-start.3
  52.8 25.6 %all-to-all-done.1 = f32[32,8,1,1024]{3,1,2,0:T(8,128)S(1)} async-done(((f32[32,8,1,1024]{3,1,2,0:T(8,128)}), f32[32,8,1,1024]{3,1,2,0:T(8,128)S(1)}, u32[]{:S(2)}, u32[]{:S(2)}) %all-to-all-start.1) | async-done | bytes 1048608 | tf_op jit(solution)/shard_map/all_to_all | solution.py:248
  78.4 0.5 fusion.2.sums_ref
  78.9 0.0 copy-done
  78.9 0.0 copy-done.1
  78.9 0.0 copy-done.2
  78.9 0.0 copy-done.3
  78.9 28.3 %shard_map.86 = (f32[128,1024]{1,0:T(8,128)S(1)}, f32[128,1024]{1,0:T(8,128)S(1)}) custom-call(f32[128,1024]{1,0:T(8,128)S(1)} %fusion.2.sums_ref, f32[128,1024]{1,0:T(8,128)S(1)} %fusion.weights_ref, f32[128,1024]{1,0:T(8,128)S(1)} %copy-done, bf16[256,192]{1,0:T(8,128)(2,1)S(1)} %copy-done.3, bf16[512,256]{1,0:T(8,128)(2,1)S(1)} %copy-done.2, ...), custom_call_target="tpu_custom_call" | custom-call | tf_op jit(solution)/shard_map/pallas_call | solution.py:210
  107.3 0.8 copy.22
  108.1 0.8 copy.23
  (1 shorter events, 0.0 us)
Async XLA Ops:
  0.6 0.7 copy-start.5
  3.5 14.4 %all-to-all-start = ((s32[32,1,8]{2,1,0:T(1,128)}), s32[32,1,8]{2,1,0:T(1,128)S(1)}, u32[]{:S(2)}, u32[]{:S(2)}) async-start(s32[32,1,8]{2,1,0:T(1,128)} %bitcast.3), calls=%async_computation | async-start | bytes 32768 | tf_op jit(solution)/shard_map/all_to_all | solution.py:248
  18.0 2.8 %copy-start.4 = (f32[128,1,1024]{2,1,0:T(1,128)S(1)}, f32[128,1,1024]{2,1,0:T(1,128)}, u32[]{:S(2)}) copy-start(f32[128,1,1024]{2,1,0:T(1,128)} %param.7) | copy-start | bytes 1572868
  18.0 30.3 %all-to-all-start.2 = ((f32[32,8,1,1024]{3,1,2,0:T(8,128)}), f32[32,8,1,1024]{3,1,2,0:T(8,128)S(1)}, u32[]{:S(2)}, u32[]{:S(2)}) async-start(f32[32,8,1,1024]{3,1,2,0:T(8,128)} %bitcast.6), calls=%async_computation.2 | async-start | bytes 2097152 | tf_op jit(solution)/shard_map/all_to_all | solution.py:248
  48.2 30.1 %all-to-all-start.1 = ((f32[32,8,1,1024]{3,1,2,0:T(8,128)}), f32[32,8,1,1024]{3,1,2,0:T(8,128)S(1)}, u32[]{:S(2)}, u32[]{:S(2)}) async-start(f32[32,8,1,1024]{3,1,2,0:T(8,128)} %bitcast.4), calls=%async_computation.1 | async-start | bytes 2097152 | tf_op jit(solution)/shard_map/all_to_all | solution.py:248
  52.7 26.2 %copy-start = (f32[128,1024]{1,0:T(8,128)S(1)}, f32[128,1024]{1,0:T(8,128)}, u32[]{:S(2)}) copy-start(f32[128,1024]{1,0:T(8,128)} %prior_ref.1) | copy-start | bytes 1572868
  52.7 26.2 %copy-start.1 = (bf16[512,256]{1,0:T(8,128)(2,1)S(1)}, bf16[512,256]{1,0:T(8,128)(2,1)}, u32[]{:S(2)}) copy-start(bf16[512,256]{1,0:T(8,128)(2,1)} %constant.31.col_low_ref) | copy-start | bytes 786436
  52.7 26.2 %copy-start.2 = (bf16[512,256]{1,0:T(8,128)(2,1)S(1)}, bf16[512,256]{1,0:T(8,128)(2,1)}, u32[]{:S(2)}) copy-start(bf16[512,256]{1,0:T(8,128)(2,1)} %constant.28.col_high_ref) | copy-start | bytes 786436
  52.7 26.2 %copy-start.3 = (bf16[256,192]{1,0:T(8,128)(2,1)S(1)}, bf16[256,192]{1,0:T(8,128)(2,1)}, u32[]{:S(2)}) copy-start(bf16[256,192]{1,0:T(8,128)(2,1)} %constant.27.row_ref) | copy-start | bytes 294916

commit v2 on v1

--- a/solution.py
+++ b/solution.py
@@ -51,24 +51,36 @@
 def solve_kernel(
     ny,
     nx,
+    slots,
     sums_ref,
     weights_ref,
+    tile_ref,
+    band_ref,
     prior_ref,
     row_ref,
     col_high_ref,
     col_low_ref,
     field_ref,
     residual_ref,
+    send_sums,
+    send_weights,
+    send_table,
+    got_sums,
+    got_weights,
+    got_table,
     pad_a,
     pad_b,
     part,
     parts,
+    route_send,
+    route_recv,
     halo_send,
     halo_recv,
     part_send,
     part_recv,
 ):
     count = ny * nx
+    blocks, groups, _ = sums_ref.shape
     rows, cols = prior_ref.shape
     width = col_high_ref.shape[1]
     ty, tx = lax.axis_index("ty"), lax.axis_index("tx")
@@ -91,9 +103,78 @@
 
     lax.fori_loop(1, count, greet, 0)
 
-    pad_a[HALF : HALF + rows, LANES : LANES + cols] = sums_ref[...]
-    root = jnp.sqrt(prior_ref[...] + weights_ref[...])
+    def dot(left, right):
+        return jnp.dot(left, right, preferred_element_type=jnp.float32)
+
+    def cross(left, right):
+        return lax.dot_general(
+            left, right, (((0,), (0,)), ((), ())), preferred_element_type=jnp.float32
+        )
+
+    def iota(shape, dim):
+        return lax.broadcasted_iota(jnp.int32, shape, dim)
+
+    def ones(mask):
+        return jnp.where(mask, 1.0, 0.0).astype(jnp.bfloat16)
+
+    tile = tile_ref[...]
+    square = (blocks, blocks)
+    down, across = iota(square, 0), iota(square, 1)
+
+    def as_column(row):
+        spread = jnp.broadcast_to(row, square)
+        return jnp.sum(jnp.where(down == across, spread, 0), axis=1, keepdims=True)
+
+    tile_column = as_column(tile)
+    same = jnp.where(tile_column == tile, 1, 0)
+    rank = jnp.sum(jnp.where(down < across, same, 0), axis=0, keepdims=True)
+    rank_column = jnp.sum(jnp.where(across < down, same, 0), axis=1, keepdims=True)
+    place = ones(iota((count * slots, blocks), 0) == tile * slots + rank)
+    owner = ones(iota((count, blocks), 0) == tile)
+    numbers = jnp.where(
+        rank_column == iota((blocks, LANES), 1), as_column(band_ref[...]) + 1, 0
+    ).astype(jnp.float32)
+    send_table[...] = dot(owner, numbers.astype(jnp.bfloat16)).reshape(count, 1, LANES)
+
+    def pack(source, target):
+        for group in range(groups):
+            high, low = halves(source[:, group, :])
+            moved = dot(place, high) + dot(place, low)
+            target[:, :, group * LANES : (group + 1) * LANES] = moved.reshape(count, slots, LANES)
+
+    pack(sums_ref, send_sums)
+    pack(weights_ref, send_weights)
+    got_table[pl.ds(me, 1)] = send_table[pl.ds(me, 1)]
+    got_sums[pl.ds(me, 1)] = send_sums[pl.ds(me, 1)]
+    got_weights[pl.ds(me, 1)] = send_weights[pl.ds(me, 1)]
+
     pl.semaphore_wait(barrier, count - 1)
+
+    def route(source, target, which, start, stop):
+        def send(index, carry):
+            hop = index // ny
+            sign = 1 - 2 * lax.rem(hop, 2)
+            other_x = lax.rem(tx + nx // 2 + nx + sign * ((hop + 1) // 2), nx)
+            other_y = lax.rem(ty + index, ny)
+
+            @pl.when(other_y * nx + other_x != me)
+            def _():
+                pltpu.make_async_remote_copy(
+                    src_ref=source.at[other_y * nx + other_x],
+                    dst_ref=target.at[me],
+                    send_sem=route_send.at[which],
+                    recv_sem=route_recv.at[which],
+                    device_id=(other_y, other_x),
+                    device_id_type=MESH,
+                ).start()
+
+            return carry
+
+        lax.fori_loop(start, stop, send, 0)
+
+    def arrived(target, which, semaphores):
+        others = target.at[pl.ds(0, count - 1)]
+        pltpu.make_async_copy(others, others, semaphores.at[which]).wait()
 
     def exchange(pad, phase):
         copies = []
@@ -117,16 +198,15 @@
             comes = (ty - dy >= 0) & (ty - dy < ny) & (tx - dx >= 0) & (tx - dx < nx)
             copies.append((copy, goes, comes))
             pl.when(goes)(copy.start)
+        return copies
+
+    def receive(copies):
         for copy, goes, comes in copies:
             pl.when(comes)(copy.wait_recv)
-        return copies
 
     def finish(copies):
         for copy, goes, comes in copies:
             pl.when(goes)(copy.wait_send)
-
-    def dot(left, right):
-        return jnp.dot(left, right, preferred_element_type=jnp.float32)
 
     def smooth(pad):
         high, low = halves(pad[...])
@@ -144,13 +224,41 @@
     def total(values):
         return jnp.sum(values, axis=(0, 1), keepdims=True)
 
+    early = count // 2
+    route(send_table, got_table, 0, 0, count)
+    route(send_sums, got_sums, 1, 0, count)
+    route(send_weights, got_weights, 2, 0, early)
+
+    arrived(got_table, 0, route_recv)
+    spread = ones(
+        iota((count, count * slots), 0) == iota((count, count * slots), 1) // slots
+    )
+    table = got_table[...].reshape(count, LANES).astype(jnp.bfloat16)
+    listed = cross(table, spread)
+    wanted = iota(listed.shape, 0) == lax.rem(iota(listed.shape, 1), slots)
+    listed = jnp.sum(jnp.where(wanted, listed, 0.0), axis=0, keepdims=True)
+    select = ones(iota((rows, count * slots), 0).astype(jnp.float32) + 1.0 == listed)
+
+    def gather(source):
+        high, low = halves(source[...].reshape(count * slots, cols))
+        return dot(select, high) + dot(select, low)
+
+    arrived(got_sums, 1, route_recv)
+    pad_a[HALF : HALF + rows, LANES : LANES + cols] = gather(got_sums)
     first = exchange(pad_a, 0)
-    r0 = sums_ref[...] / root
-    u = root * smooth(pad_a)
+    route(send_weights, got_weights, 2, early, count)
+    receive(first)
+    field_ref[...] = smooth(pad_a)
+
+    arrived(got_weights, 2, route_recv)
+    root = jnp.sqrt(prior_ref[...] + gather(got_weights))
+    r0 = pad_a[HALF : HALF + rows, LANES : LANES + cols] / root
+    u = root * field_ref[...]
     pad_b[HALF : HALF + rows, LANES : LANES + cols] = root * u
     second = exchange(pad_b, 1)
     rr, ru = total(r0 * r0), total(r0 * u)
     own = jnp.where(rr > 0.0, ru / rr, 0.0)
+    receive(second)
     z = root * smooth(pad_b)
     q = own * r0 - u
     g = own * u - z
@@ -166,16 +274,15 @@
         pltpu.make_async_remote_copy(
             src_ref=part,
             dst_ref=parts.at[me],
-            send_sem=part_send,
-            recv_sem=part_recv,
+            send_sem=part_send.at[0],
+            recv_sem=part_recv.at[0],
             device_id=(other // nx, lax.rem(other, nx)),
             device_id_type=MESH,
         ).start()
         return carry
 
     lax.fori_loop(1, count, tell, 0)
-    everyone = parts.at[pl.ds(0, count - 1)]
-    pltpu.make_async_copy(everyone, everyone, part_recv).wait()
+    arrived(parts, 0, part_recv)
 
     table = parts[...].reshape(count, LANES)
     rr_d, ru_d, qq_d, qg_d, rg_d = [table[:, i : i + 1] for i in range(5)]
@@ -196,72 +303,58 @@
 
     finish(first)
     finish(second)
-    pltpu.make_async_copy(everyone, everyone, part_send).wait()
-
-
-def solve(ny, nx, cell_sums, cell_weights, prior_weight):
-    rows, cols = prior_weight.shape
+    arrived(send_table, 0, route_send)
+    arrived(send_sums, 1, route_send)
+    arrived(send_weights, 2, route_send)
+    arrived(parts, 0, part_send)
+
+
+def shards(block_sums, block_weights, block_tile, block_row, prior_weight):
+    ny, nx = lax.axis_size("ty"), lax.axis_size("tx")
     count = ny * nx
-    width = 2 * LANES
-    matrices = kernel_matrices(rows, width)
+    blocks, band, cols = block_sums.shape
+    rows = prior_weight.shape[0]
+    slots = 2 * blocks // count
+    matrices = kernel_matrices(rows, 2 * LANES)
     vmem = pl.BlockSpec(memory_space=pltpu.VMEM)
     shape = jax.ShapeDtypeStruct((rows, cols), jnp.float32)
     padded = pltpu.VMEM((rows + 2 * HALF, cols + 2 * LANES), jnp.float32)
+    chunks = pltpu.VMEM((count, slots, cols), jnp.float32)
+    lines = pltpu.VMEM((count, 1, LANES), jnp.float32)
     return pl.pallas_call(
-        functools.partial(solve_kernel, ny, nx),
+        functools.partial(solve_kernel, ny, nx, slots),
         out_shape=(shape, shape),
-        in_specs=[vmem] * 6,
+        in_specs=[vmem] * 8,
         out_specs=(vmem, vmem),
         scratch_shapes=[
+            chunks,
+            chunks,
+            lines,
+            chunks,
+            chunks,
+            lines,
             padded,
             padded,
             pltpu.VMEM((1, LANES), jnp.float32),
-            pltpu.VMEM((count, 1, LANES), jnp.float32),
+            lines,
+            pltpu.SemaphoreType.DMA((3,)),
+            pltpu.SemaphoreType.DMA((3,)),
             pltpu.SemaphoreType.DMA((2, 8)),
             pltpu.SemaphoreType.DMA((2, 8)),
-            pltpu.SemaphoreType.DMA,
-            pltpu.SemaphoreType.DMA,
+            pltpu.SemaphoreType.DMA((1,)),
+            pltpu.SemaphoreType.DMA((1,)),
         ],
         compiler_params=pltpu.CompilerParams(
-            collective_id=0, has_side_effects=True, vmem_limit_bytes=40 * 2**20
+            collective_id=0, has_side_effects=True, vmem_limit_bytes=48 * 2**20
         ),
-    )(cell_sums, cell_weights, prior_weight, *matrices)
-
-
-def shards(block_sums, block_weights, block_tile, block_row, prior_weight):
-    ny, nx = lax.axis_size("ty"), lax.axis_size("tx")
-    devices = ny * nx
-    blocks, band, cols = block_sums.shape
-    rows = prior_weight.shape[0]
-    slots = 2 * blocks // devices
-    target = block_tile[:, 0]
-    owners = (target[:, None] == jnp.arange(devices, dtype=jnp.int32)[None, :]).astype(jnp.int32)
-    rank = jnp.sum((jnp.cumsum(owners, axis=0) - 1) * owners, axis=1)
-    position = target * slots + rank
-    send_sums = jnp.zeros((devices * slots, band, cols), jnp.float32).at[position].set(block_sums)
-    send_weights = (
-        jnp.zeros((devices * slots, band, cols), jnp.float32).at[position].set(block_weights)
+    )(
+        block_sums.reshape(blocks * band, cols // LANES, LANES),
+        block_weights.reshape(blocks * band, cols // LANES, LANES),
+        block_tile.reshape(1, blocks),
+        block_row.reshape(1, blocks),
+        prior_weight,
+        *matrices,
     )
-    send_rows = jnp.zeros((devices * slots,), jnp.int32).at[position].set(block_row)
-
-    def swap(values):
-        return lax.all_to_all(values, ("ty", "tx"), split_axis=0, concat_axis=0, tiled=True)
-
-    got_sums = swap(send_sums.reshape(devices, slots, band, cols))
-    got_weights = swap(send_weights.reshape(devices, slots, band, cols))
-    got_rows = swap(send_rows.reshape(devices, slots))
-    received = devices * slots
-    got_rows = got_rows.reshape(received)
-    select = (jnp.arange(rows // band, dtype=jnp.int32)[:, None] == got_rows[None, :]).astype(
-        jnp.float32
-    )
-    cell_sums = jnp.dot(
-        select, got_sums.reshape(received, band * cols), precision=lax.Precision.HIGHEST
-    )
-    cell_weights = jnp.dot(
-        select, got_weights.reshape(received, band * cols), precision=lax.Precision.HIGHEST
-    )
-    return solve(ny, nx, cell_sums, cell_weights, prior_weight)
 
 
 def solution(mesh):

time: 109 us -> 80.6 us (0.74)
  waiting for transfers between devices: 55.4 us -> 0 us
  Pallas kernels: 28.3 us -> 71.4 us
  starting transfers between devices: 12.7 us -> 0 us
  local copies, waits for them, and re-layouts: 9.46 us -> 8.17 us
  other arithmetic: 1.12 us -> 0 us
    all_to_all x3 -> x0, waiting for transfers between devices: 55.4 us -> none  [swap(): lax.all_to_all(values, ('ty', 'tx'), split_axis=0, concat_axis=0, tiled=T...]
    pallas_call x1, Pallas kernels: 28.3 us -> 71.4 us  [shards(): pl.pallas_call(functools.partial(solve_kernel, ny, nx, slots), out_shape=...]
    all_to_all x3 -> x0, starting transfers between devices: 12.7 us -> none  [swap(): lax.all_to_all(values, ('ty', 'tx'), split_axis=0, concat_axis=0, tiled=T...]
    unnamed x14 -> x18, local copies, waits for them, and re-layouts: 2.27 us -> 8.17 us
    scatter x3 -> x0, local copies, waits for them, and re-layouts: 5.9 us -> none  [the longest x2 4.79 us: shards(): jnp.zeros((devices * slots, band, cols), jnp.float32).at[position]]
    all_to_all x2 -> x0, local copies, waits for them, and re-layouts: 1.21 us -> none  [swap(): lax.all_to_all(values, ('ty', 'tx'), split_axis=0, concat_axis=0, tiled=T...]
  transfers between devices with their start and end apart: 3 -> 0, of which waited for: 3 -> 0; matrix products, arithmetic and copies ran while one was open for 6% -> 0% of each run, Pallas kernels for 0% -> 0%
where the time goes in v2:
time: 80.6 us; the launch traced here: 80.2 us
  Pallas kernels  71.4 us (89%)
  local copies, waits for them, and re-layouts  8.17 us (10%)
    pallas_call x1, Pallas kernels, shards(): pl.pallas_call(functools.partial(solve_kernel, ny, nx, slots), out_shape=...  71.4 us
    unnamed x18, local copies, waits for them, and re-layouts  8.17 us

profile of v2, /device:TPU:0, one launch (start us, length us, event | category | flops | bytes accessed | tf_op | source)
XLA Modules:
  0.0 80.2 jit_solution(14711653117696734803)
XLA Ops:
  0.6 0.0 copy-start.6
  0.6 0.0 copy-start.7
  0.7 0.6 copy-done.6
  1.3 0.0 copy-done.7
  1.3 0.0 copy-start
  1.3 1.0 %copy-done = f32[128,1,1024]{2,1,0:T(1,128)S(1)} copy-done((f32[128,1,1024]{2,1,0:T(1,128)S(1)}, f32[128,1,1024]{2,1,0:T(1,128)}, u32[]{:S(2)}) %copy-start) | copy-done | bytes 524312
  2.3 0.0 copy-start.1
  2.3 1.0 %copy-done.1 = f32[128,1,1024]{2,1,0:T(1,128)S(1)} copy-done((f32[128,1,1024]{2,1,0:T(1,128)S(1)}, f32[128,1,1024]{2,1,0:T(1,128)}, u32[]{:S(2)}) %copy-start.1) | copy-done | bytes 524312
  3.4 0.0 copy-start.2
  3.4 1.0 %copy-done.2 = f32[128,1024]{1,0:T(8,128)S(1)} copy-done((f32[128,1024]{1,0:T(8,128)S(1)}, f32[128,1024]{1,0:T(8,128)}, u32[]{:S(2)}) %copy-start.2) | copy-done | bytes 524312
  4.4 0.0 copy-start.3
  4.4 0.9 %copy-done.3 = bf16[512,256]{1,0:T(8,128)(2,1)S(1)} copy-done((bf16[512,256]{1,0:T(8,128)(2,1)S(1)}, bf16[512,256]{1,0:T(8,128)(2,1)}, u32[]{:S(2)}) %copy-start.3) | copy-done | bytes 262168
  5.4 0.0 copy-start.4
  5.4 0.9 %copy-done.4 = bf16[512,256]{1,0:T(8,128)(2,1)S(1)} copy-done((bf16[512,256]{1,0:T(8,128)(2,1)S(1)}, bf16[512,256]{1,0:T(8,128)(2,1)}, u32[]{:S(2)}) %copy-start.4) | copy-done | bytes 262168
  6.3 0.0 copy-start.5
  6.3 0.9 %copy-done.5 = bf16[256,192]{1,0:T(8,128)(2,1)S(1)} copy-done((bf16[256,192]{1,0:T(8,128)(2,1)S(1)}, bf16[256,192]{1,0:T(8,128)(2,1)}, u32[]{:S(2)}) %copy-start.5) | copy-done | bytes 98328
  7.2 71.4 %shard_map.86 = (f32[128,1024]{1,0:T(8,128)S(1)}, f32[128,1024]{1,0:T(8,128)S(1)}) custom-call(f32[128,8,128]{2,1,0:T(8,128)S(1)} %bitcast.4, f32[128,8,128]{2,1,0:T(8,128)S(1)} %bitcast.5, s32[1,128]{1,0:T(1,128)S(1)} %bitcast.6, s32[1,128]{1,0:T(1,128)S(1)} %bitcast.7, f32[128,1024]{1,0:T(8,128)S(1)} %copy-done.2, bf16[256,192]{1,0:T(8,128)(2,1)S(1)} %copy-done.5, ...), custom_call_target="tpu_custom_call" | custom-call | tf_op jit(solution)/shard_map/pallas_call | solution.py:324
  78.7 0.8 copy.11
  79.5 0.8 copy.12
Async XLA Ops:
  0.6 0.7 copy-start.6
  0.6 0.7 copy-start.7
  1.3 1.0 %copy-start = (f32[128,1,1024]{2,1,0:T(1,128)S(1)}, f32[128,1,1024]{2,1,0:T(1,128)}, u32[]{:S(2)}) copy-start(f32[128,1,1024]{2,1,0:T(1,128)} %param.7) | copy-start | bytes 1572868
  2.3 1.0 %copy-start.1 = (f32[128,1,1024]{2,1,0:T(1,128)S(1)}, f32[128,1,1024]{2,1,0:T(1,128)}, u32[]{:S(2)}) copy-start(f32[128,1,1024]{2,1,0:T(1,128)} %param.8) | copy-start | bytes 1572868
  3.4 1.0 %copy-start.2 = (f32[128,1024]{1,0:T(8,128)S(1)}, f32[128,1024]{1,0:T(8,128)}, u32[]{:S(2)}) copy-start(f32[128,1024]{1,0:T(8,128)} %prior_ref.1) | copy-start | bytes 1572868
  4.4 0.9 %copy-start.3 = (bf16[512,256]{1,0:T(8,128)(2,1)S(1)}, bf16[512,256]{1,0:T(8,128)(2,1)}, u32[]{:S(2)}) copy-start(bf16[512,256]{1,0:T(8,128)(2,1)} %constant.14.col_low_ref) | copy-start | bytes 786436
  5.4 0.9 %copy-start.4 = (bf16[512,256]{1,0:T(8,128)(2,1)S(1)}, bf16[512,256]{1,0:T(8,128)(2,1)}, u32[]{:S(2)}) copy-start(bf16[512,256]{1,0:T(8,128)(2,1)} %constant.11.col_high_ref) | copy-start | bytes 786436
  6.3 0.9 %copy-start.5 = (bf16[256,192]{1,0:T(8,128)(2,1)S(1)}, bf16[256,192]{1,0:T(8,128)(2,1)}, u32[]{:S(2)}) copy-start(bf16[256,192]{1,0:T(8,128)(2,1)} %constant.10.row_ref) | copy-start | bytes 294916

commit v3 on v2

--- a/solution.py
+++ b/solution.py
@@ -10,6 +10,7 @@
 
 HALF = 32
 LANES = 128
+PIECES = 2
 MESH = pl.DeviceIdType.MESH
 
 
@@ -52,16 +53,26 @@
     ny,
     nx,
     slots,
+    tile_ref,
+    band_ref,
+    sums_hbm,
+    weights_hbm,
+    prior_hbm,
+    row_hbm,
+    col_high_hbm,
+    col_low_hbm,
+    r0_ref,
+    u_ref,
+    z_ref,
+    scalars_ref,
     sums_ref,
     weights_ref,
-    tile_ref,
-    band_ref,
     prior_ref,
     row_ref,
     col_high_ref,
     col_low_ref,
-    field_ref,
-    residual_ref,
+    root_ref,
+    load_sem,
     send_sums,
     send_weights,
     send_table,
@@ -86,22 +97,49 @@
     ty, tx = lax.axis_index("ty"), lax.axis_index("tx")
     me = ty * nx + tx
 
+    def device(index):
+        hop = index // ny
+        sign = 1 - 2 * lax.rem(hop, 2)
+        other_x = lax.rem(tx + nx // 2 + nx + sign * ((hop + 1) // 2), nx)
+        return lax.rem(ty + ny // 2 + index, ny), other_x
+
     barrier = pltpu.get_barrier_semaphore()
 
+    def greet(index, carry):
+        other_y, other_x = device(index)
+
+        @pl.when(other_y * nx + other_x != me)
+        def _():
+            pl.semaphore_signal(
+                barrier, inc=1, device_id=(other_y, other_x), device_id_type=MESH
+            )
+
+        return carry
+
+    loads = [
+        pltpu.make_async_copy(source, target, load_sem.at[index])
+        for index, (source, target) in enumerate(
+            (
+                (sums_hbm, sums_ref),
+                (weights_hbm, weights_ref),
+                (row_hbm, row_ref),
+                (col_high_hbm, col_high_ref),
+                (col_low_hbm, col_low_ref),
+                (prior_hbm, prior_ref),
+            )
+        )
+    ]
+    loads[0].start()
+    loads[1].start()
     for pad in (pad_a, pad_b):
         pad[0:HALF, :] = jnp.zeros((HALF, cols + 2 * LANES), jnp.float32)
         pad[HALF + rows :, :] = jnp.zeros((HALF, cols + 2 * LANES), jnp.float32)
         pad[HALF : HALF + rows, 0:LANES] = jnp.zeros((rows, LANES), jnp.float32)
         pad[HALF : HALF + rows, LANES + cols :] = jnp.zeros((rows, LANES), jnp.float32)
 
-    def greet(step, carry):
-        other = lax.rem(me + step, count)
-        pl.semaphore_signal(
-            barrier, inc=1, device_id=(other // nx, lax.rem(other, nx)), device_id_type=MESH
-        )
-        return carry
-
-    lax.fori_loop(1, count, greet, 0)
+    lax.fori_loop(0, count, greet, 0)
+    for load in loads[2:]:
+        load.start()
 
     def dot(left, right):
         return jnp.dot(left, right, preferred_element_type=jnp.float32)
@@ -142,26 +180,16 @@
             moved = dot(place, high) + dot(place, low)
             target[:, :, group * LANES : (group + 1) * LANES] = moved.reshape(count, slots, LANES)
 
-    pack(sums_ref, send_sums)
-    pack(weights_ref, send_weights)
-    got_table[pl.ds(me, 1)] = send_table[pl.ds(me, 1)]
-    got_sums[pl.ds(me, 1)] = send_sums[pl.ds(me, 1)]
-    got_weights[pl.ds(me, 1)] = send_weights[pl.ds(me, 1)]
-
-    pl.semaphore_wait(barrier, count - 1)
-
-    def route(source, target, which, start, stop):
+    def route(source, target, which, window=None):
         def send(index, carry):
-            hop = index // ny
-            sign = 1 - 2 * lax.rem(hop, 2)
-            other_x = lax.rem(tx + nx // 2 + nx + sign * ((hop + 1) // 2), nx)
-            other_y = lax.rem(ty + index, ny)
-
-            @pl.when(other_y * nx + other_x != me)
+            other_y, other_x = device(index)
+            other = other_y * nx + other_x
+
+            @pl.when(other != me)
             def _():
                 pltpu.make_async_remote_copy(
-                    src_ref=source.at[other_y * nx + other_x],
-                    dst_ref=target.at[me],
+                    src_ref=source.at[other] if window is None else source.at[other, :, window],
+                    dst_ref=target.at[me] if window is None else target.at[me, :, window],
                     send_sem=route_send.at[which],
                     recv_sem=route_recv.at[which],
                     device_id=(other_y, other_x),
@@ -170,21 +198,28 @@
 
             return carry
 
-        lax.fori_loop(start, stop, send, 0)
-
-    def arrived(target, which, semaphores):
-        others = target.at[pl.ds(0, count - 1)]
+        lax.fori_loop(0, count, send, 0)
+
+    def arrived(target, which, semaphores, window=None):
+        first = pl.ds(0, count - 1)
+        others = target.at[first] if window is None else target.at[first, :, window]
         pltpu.make_async_copy(others, others, semaphores.at[which]).wait()
 
-    def exchange(pad, phase):
+    def exchange(pad, phase, piece=0, count_of=1):
+        size = cols // count_of
         copies = []
         for index, (dy, dx) in enumerate(directions()):
+            if (dx < 0 and piece > 0) or (dx > 0 and piece + 1 < count_of):
+                continue
+            middle = pl.ds(LANES + piece * size, size)
             copy = pltpu.make_async_remote_copy(
                 src_ref=pad.at[
-                    span(dy, rows, HALF, HALF, True), span(dx, cols, LANES, LANES, True)
+                    span(dy, rows, HALF, HALF, True),
+                    span(dx, cols, LANES, LANES, True) if dx else middle,
                 ],
                 dst_ref=pad.at[
-                    span(dy, rows, HALF, HALF, False), span(dx, cols, LANES, LANES, False)
+                    span(dy, rows, HALF, HALF, False),
+                    span(dx, cols, LANES, LANES, False) if dx else middle,
                 ],
                 send_sem=halo_send.at[phase, index],
                 recv_sem=halo_recv.at[phase, index],
@@ -224,10 +259,19 @@
     def total(values):
         return jnp.sum(values, axis=(0, 1), keepdims=True)
 
-    early = count // 2
-    route(send_table, got_table, 0, 0, count)
-    route(send_sums, got_sums, 1, 0, count)
-    route(send_weights, got_weights, 2, 0, early)
+    size = cols // PIECES
+    windows = [pl.ds(piece * size, size) for piece in range(PIECES)]
+    loads[0].wait()
+    pack(sums_ref, send_sums)
+    pl.semaphore_wait(barrier, count - 1)
+    route(send_table, got_table, 0)
+    route(send_sums, got_sums, 1)
+    loads[1].wait()
+    pack(weights_ref, send_weights)
+    route(send_weights, got_weights, 2, windows[0])
+    got_table[pl.ds(me, 1)] = send_table[pl.ds(me, 1)]
+    got_sums[pl.ds(me, 1)] = send_sums[pl.ds(me, 1)]
+    got_weights[pl.ds(me, 1)] = send_weights[pl.ds(me, 1)]
 
     arrived(got_table, 0, route_recv)
     spread = ones(
@@ -239,27 +283,38 @@
     listed = jnp.sum(jnp.where(wanted, listed, 0.0), axis=0, keepdims=True)
     select = ones(iota((rows, count * slots), 0).astype(jnp.float32) + 1.0 == listed)
 
-    def gather(source):
-        high, low = halves(source[...].reshape(count * slots, cols))
+    def gather(values):
+        high, low = halves(values.reshape(count * slots, values.shape[-1]))
         return dot(select, high) + dot(select, low)
 
     arrived(got_sums, 1, route_recv)
-    pad_a[HALF : HALF + rows, LANES : LANES + cols] = gather(got_sums)
+    pad_a[HALF : HALF + rows, LANES : LANES + cols] = gather(got_sums[...])
     first = exchange(pad_a, 0)
-    route(send_weights, got_weights, 2, early, count)
+    for piece in range(1, PIECES):
+        route(send_weights, got_weights, 2 + piece, windows[piece])
+    for load in loads[2:]:
+        load.wait()
     receive(first)
-    field_ref[...] = smooth(pad_a)
-
-    arrived(got_weights, 2, route_recv)
-    root = jnp.sqrt(prior_ref[...] + gather(got_weights))
-    r0 = pad_a[HALF : HALF + rows, LANES : LANES + cols] / root
-    u = root * field_ref[...]
-    pad_b[HALF : HALF + rows, LANES : LANES + cols] = root * u
-    second = exchange(pad_b, 1)
+    u_ref[...] = smooth(pad_a)
+
+    second = []
+    for piece, window in enumerate(windows):
+        left = piece * size
+        inner = slice(LANES + left, LANES + left + size)
+        arrived(got_weights, 2 + piece, route_recv, window)
+        root = jnp.sqrt(prior_ref[:, window] + gather(got_weights[:, :, window]))
+        root_ref[:, window] = root
+        r0_ref[:, window] = pad_a[HALF : HALF + rows, inner] / root
+        u = root * u_ref[:, window]
+        u_ref[:, window] = u
+        pad_b[HALF : HALF + rows, inner] = root * u
+        second += exchange(pad_b, 1 + piece, piece, PIECES)
+    r0, u = r0_ref[...], u_ref[...]
     rr, ru = total(r0 * r0), total(r0 * u)
     own = jnp.where(rr > 0.0, ru / rr, 0.0)
     receive(second)
-    z = root * smooth(pad_b)
+    z = root_ref[...] * smooth(pad_b)
+    z_ref[...] = z
     q = own * r0 - u
     g = own * u - z
     lane = lax.broadcasted_iota(jnp.int32, (1, LANES), 1)
@@ -269,19 +324,23 @@
     part[...] = packed
     parts[pl.ds(me, 1), 0, :] = packed
 
-    def tell(step, carry):
-        other = lax.rem(me + step, count)
-        pltpu.make_async_remote_copy(
-            src_ref=part,
-            dst_ref=parts.at[me],
-            send_sem=part_send.at[0],
-            recv_sem=part_recv.at[0],
-            device_id=(other // nx, lax.rem(other, nx)),
-            device_id_type=MESH,
-        ).start()
+    def tell(index, carry):
+        other_y, other_x = device(index)
+
+        @pl.when(other_y * nx + other_x != me)
+        def _():
+            pltpu.make_async_remote_copy(
+                src_ref=part,
+                dst_ref=parts.at[me],
+                send_sem=part_send.at[0],
+                recv_sem=part_recv.at[0],
+                device_id=(other_y, other_x),
+                device_id_type=MESH,
+            ).start()
+
         return carry
 
-    lax.fori_loop(1, count, tell, 0)
+    lax.fori_loop(0, count, tell, 0)
     arrived(parts, 0, part_recv)
 
     table = parts[...].reshape(count, LANES)
@@ -295,17 +354,17 @@
     norm = alpha0 * alpha0 * qq
     beta = norm / rr
     alpha1 = norm / (alpha0 * alpha0 * (0.5 * qq + qg) - beta * norm / alpha0)
-    q = mu * r0 - u
-    r1 = alpha0 * q
-    field_ref[...] = alpha0 * r0 + alpha1 * (r1 + beta * r0)
-    along = alpha0 * (0.5 * q + mu * u - z) + beta * (0.5 * r0 + u)
-    residual_ref[...] = r1 - alpha1 * along
+    packed = jnp.zeros((1, LANES), jnp.float32)
+    for index, value in enumerate((alpha0, alpha1, beta, mu)):
+        packed = jnp.where(lane == index, value, packed)
+    scalars_ref[...] = packed
 
     finish(first)
     finish(second)
     arrived(send_table, 0, route_send)
     arrived(send_sums, 1, route_send)
-    arrived(send_weights, 2, route_send)
+    for piece, window in enumerate(windows):
+        arrived(send_weights, 2 + piece, route_send, window)
     arrived(parts, 0, part_send)
 
 
@@ -321,12 +380,20 @@
     padded = pltpu.VMEM((rows + 2 * HALF, cols + 2 * LANES), jnp.float32)
     chunks = pltpu.VMEM((count, slots, cols), jnp.float32)
     lines = pltpu.VMEM((count, 1, LANES), jnp.float32)
-    return pl.pallas_call(
+    hbm = pl.BlockSpec(memory_space=pltpu.HBM)
+    inputs = pltpu.VMEM((blocks * band, cols // LANES, LANES), jnp.float32)
+    r0, u, z, scalars = pl.pallas_call(
         functools.partial(solve_kernel, ny, nx, slots),
-        out_shape=(shape, shape),
-        in_specs=[vmem] * 8,
-        out_specs=(vmem, vmem),
+        out_shape=(shape, shape, shape, jax.ShapeDtypeStruct((1, LANES), jnp.float32)),
+        in_specs=[vmem] * 2 + [hbm] * 6,
+        out_specs=(vmem,) * 4,
         scratch_shapes=[
+            inputs,
+            inputs,
+            pltpu.VMEM((rows, cols), jnp.float32),
+            *[pltpu.VMEM(matrix.shape, matrix.dtype) for matrix in matrices],
+            pltpu.VMEM((rows, cols), jnp.float32),
+            pltpu.SemaphoreType.DMA((6,)),
             chunks,
             chunks,
             lines,
@@ -337,10 +404,10 @@
             padded,
             pltpu.VMEM((1, LANES), jnp.float32),
             lines,
-            pltpu.SemaphoreType.DMA((3,)),
-            pltpu.SemaphoreType.DMA((3,)),
-            pltpu.SemaphoreType.DMA((2, 8)),
-            pltpu.SemaphoreType.DMA((2, 8)),
+            pltpu.SemaphoreType.DMA((2 + PIECES,)),
+            pltpu.SemaphoreType.DMA((2 + PIECES,)),
+            pltpu.SemaphoreType.DMA((1 + PIECES, 8)),
+            pltpu.SemaphoreType.DMA((1 + PIECES, 8)),
             pltpu.SemaphoreType.DMA((1,)),
             pltpu.SemaphoreType.DMA((1,)),
         ],
@@ -348,13 +415,18 @@
             collective_id=0, has_side_effects=True, vmem_limit_bytes=48 * 2**20
         ),
     )(
+        block_tile.reshape(1, blocks),
+        block_row.reshape(1, blocks),
         block_sums.reshape(blocks * band, cols // LANES, LANES),
         block_weights.reshape(blocks * band, cols // LANES, LANES),
-        block_tile.reshape(1, blocks),
-        block_row.reshape(1, blocks),
         prior_weight,
         *matrices,
     )
+    alpha0, alpha1, beta, mu = [scalars[0, index] for index in range(4)]
+    q = mu * r0 - u
+    r1 = alpha0 * q
+    along = alpha0 * (0.5 * q + mu * u - z) + beta * (0.5 * r0 + u)
+    return alpha0 * r0 + alpha1 * (r1 + beta * r0), r1 - alpha1 * along
 
 
 def solution(mesh):

time: 80.6 us -> 80.1 us (level)
  other arithmetic: 0 us -> 3.74 us
  Pallas kernels: 71.4 us -> 68.1 us
  local copies, waits for them, and re-layouts: 8.17 us -> 7.23 us
    sub x0 -> x1, other arithmetic: none -> 3.74 us  [shards(): return (alpha0 * r0 + alpha1 * (r1 + beta * r0), r1 - alpha1 * along)]
    pallas_call x1, Pallas kernels: 71.4 us -> 68.1 us  [shards(): pl.pallas_call(functools.partial(solve_kernel, ny, nx, slots), out_shape=...]
    unnamed x18 -> x16, local copies, waits for them, and re-layouts: 8.17 us -> 6.58 us
where the time goes in v3:
time: 80.1 us; the launch traced here: 79.7 us
  Pallas kernels  68.1 us (85%)
  local copies, waits for them, and re-layouts  7.23 us (9%)
  other arithmetic  3.74 us (5%)
    pallas_call x1, Pallas kernels, shards(): pl.pallas_call(functools.partial(solve_kernel, ny, nx, slots), out_shape=...  68.1 us
    unnamed x16, local copies, waits for them, and re-layouts  6.58 us
    sub x1, other arithmetic, shards(): return (alpha0 * r0 + alpha1 * (r1 + beta * r0), r1 - alpha1 * along)  3.74 us

profile of v3, /device:TPU:0, one launch (start us, length us, event | category | flops | bytes accessed | tf_op | source)
XLA Modules:
  0.0 79.7 jit_solution(1267137005568707639)
XLA Ops:
  0.6 0.0 copy-start.6
  0.6 0.0 copy-start.7
  0.7 0.6 copy-done.6
  1.3 0.0 copy-done.7
  1.3 0.0 copy-start
  1.3 1.0 %copy-done = f32[128,1,1024]{2,1,0:T(1,128)S(1)} copy-done((f32[128,1,1024]{2,1,0:T(1,128)S(1)}, f32[128,1,1024]{2,1,0:T(1,128)}, u32[]{:S(2)}) %copy-start) | copy-done | bytes 524312
  2.3 0.0 copy-start.1
  2.3 1.0 %copy-done.1 = f32[128,1,1024]{2,1,0:T(1,128)S(1)} copy-done((f32[128,1,1024]{2,1,0:T(1,128)S(1)}, f32[128,1,1024]{2,1,0:T(1,128)}, u32[]{:S(2)}) %copy-start.1) | copy-done | bytes 524312
  3.4 0.0 copy-start.2
  3.4 1.0 %copy-done.2 = f32[128,1024]{1,0:T(8,128)S(1)} copy-done((f32[128,1024]{1,0:T(8,128)S(1)}, f32[128,1024]{1,0:T(8,128)}, u32[]{:S(2)}) %copy-start.2) | copy-done | bytes 524312
  4.4 0.0 copy-start.3
  4.4 0.9 %copy-done.3 = bf16[512,256]{1,0:T(8,128)(2,1)S(1)} copy-done((bf16[512,256]{1,0:T(8,128)(2,1)S(1)}, bf16[512,256]{1,0:T(8,128)(2,1)}, u32[]{:S(2)}) %copy-start.3) | copy-done | bytes 262168
  5.4 0.0 copy-start.4
  5.4 0.9 %copy-done.4 = bf16[512,256]{1,0:T(8,128)(2,1)S(1)} copy-done((bf16[512,256]{1,0:T(8,128)(2,1)S(1)}, bf16[512,256]{1,0:T(8,128)(2,1)}, u32[]{:S(2)}) %copy-start.4) | copy-done | bytes 262168
  6.3 0.0 copy-start.5
  6.3 0.9 %copy-done.5 = bf16[256,192]{1,0:T(8,128)(2,1)S(1)} copy-done((bf16[256,192]{1,0:T(8,128)(2,1)S(1)}, bf16[256,192]{1,0:T(8,128)(2,1)}, u32[]{:S(2)}) %copy-start.5) | copy-done | bytes 98328
  7.2 68.1 %shard_map.86 = (f32[128,1024]{1,0:T(8,128)S(1)}, f32[128,1024]{1,0:T(8,128)S(1)}, f32[128,1024]{1,0:T(8,128)S(1)}, f32[1,128]{1,0:T(1,128)S(1)}) custom-call(s32[1,128]{1,0:T(1,128)S(1)} %bitcast.10, s32[1,128]{1,0:T(1,128)S(1)} %bitcast.11, f32[128,8,128]{2,1,0:T(8,128)S(1)} %bitcast.8, f32[128,8,128]{2,1,0:T(8,128)S(1)} %bitcast.9, ...), custom_call_target="tpu_custom_call" | custom-call | tf_op jit(solution)/shard_map/pallas_call | solution.py:385
  75.3 0.6 fusion.1
  76.0 3.7 %multiply_subtract_fusion = (f32[128,1024]{1,0:T(8,128)}, f32[128,1024]{1,0:T(8,128)}) fusion(f32[128,1024]{1,0:T(8,128)S(1)} %get-tuple-element.8, f32[128,1024]{1,0:T(8,128)S(1)} %get-tuple-element.7, f32[128,1024]{1,0:T(8,128)S(1)} %get-tuple-element.9, f32[]{:T(128)} %bitcast.7, f32[]{:T(128)} %bitcast.6, f32[]{:T(128)} %bitcast.5, f32[]{:T(128)} %bitcast.4), kind=kLoop, calls=%fused_computation | loop fusion | flops 2490368 | bytes 2621456 | tf_op jit(solution)/shard_map/sub | solution.py:429
Async XLA Ops:
  0.6 0.7 copy-start.6
  0.6 0.7 copy-start.7
  1.3 1.0 %copy-start = (f32[128,1,1024]{2,1,0:T(1,128)S(1)}, f32[128,1,1024]{2,1,0:T(1,128)}, u32[]{:S(2)}) copy-start(f32[128,1,1024]{2,1,0:T(1,128)} %param.7) | copy-start | bytes 1572868
  2.3 1.0 %copy-start.1 = (f32[128,1,1024]{2,1,0:T(1,128)S(1)}, f32[128,1,1024]{2,1,0:T(1,128)}, u32[]{:S(2)}) copy-start(f32[128,1,1024]{2,1,0:T(1,128)} %param.8) | copy-start | bytes 1572868
  3.4 1.0 %copy-start.2 = (f32[128,1024]{1,0:T(8,128)S(1)}, f32[128,1024]{1,0:T(8,128)}, u32[]{:S(2)}) copy-start(f32[128,1024]{1,0:T(8,128)} %prior_hbm.1) | copy-start | bytes 1572868
  4.4 0.9 %copy-start.3 = (bf16[512,256]{1,0:T(8,128)(2,1)S(1)}, bf16[512,256]{1,0:T(8,128)(2,1)}, u32[]{:S(2)}) copy-start(bf16[512,256]{1,0:T(8,128)(2,1)} %constant.16.col_low_hbm) | copy-start | bytes 786436
  5.4 0.9 %copy-start.4 = (bf16[512,256]{1,0:T(8,128)(2,1)S(1)}, bf16[512,256]{1,0:T(8,128)(2,1)}, u32[]{:S(2)}) copy-start(bf16[512,256]{1,0:T(8,128)(2,1)} %constant.13.col_high_hbm) | copy-start | bytes 786436
  6.3 0.9 %copy-start.5 = (bf16[256,192]{1,0:T(8,128)(2,1)S(1)}, bf16[256,192]{1,0:T(8,128)(2,1)}, u32[]{:S(2)}) copy-start(bf16[256,192]{1,0:T(8,128)(2,1)} %constant.12.row_hbm) | copy-start | bytes 294916

commit v4 on v3

--- a/solution.py
+++ b/solution.py
@@ -10,7 +10,8 @@
 
 HALF = 32
 LANES = 128
-PIECES = 2
+PIECES = 4
+LIMIT = 60 * 1024 * 1024
 MESH = pl.DeviceIdType.MESH
 
 
@@ -61,10 +62,8 @@
     row_hbm,
     col_high_hbm,
     col_low_hbm,
-    r0_ref,
-    u_ref,
-    z_ref,
-    scalars_ref,
+    field_ref,
+    residual_ref,
     sums_ref,
     weights_ref,
     prior_ref,
@@ -72,6 +71,8 @@
     col_high_ref,
     col_low_ref,
     root_ref,
+    r0_ref,
+    u_ref,
     load_sem,
     send_sums,
     send_weights,
@@ -314,7 +315,6 @@
     own = jnp.where(rr > 0.0, ru / rr, 0.0)
     receive(second)
     z = root_ref[...] * smooth(pad_b)
-    z_ref[...] = z
     q = own * r0 - u
     g = own * u - z
     lane = lax.broadcasted_iota(jnp.int32, (1, LANES), 1)
@@ -354,10 +354,11 @@
     norm = alpha0 * alpha0 * qq
     beta = norm / rr
     alpha1 = norm / (alpha0 * alpha0 * (0.5 * qq + qg) - beta * norm / alpha0)
-    packed = jnp.zeros((1, LANES), jnp.float32)
-    for index, value in enumerate((alpha0, alpha1, beta, mu)):
-        packed = jnp.where(lane == index, value, packed)
-    scalars_ref[...] = packed
+    q = mu * r0 - u
+    r1 = alpha0 * q
+    field_ref[...] = alpha0 * r0 + alpha1 * (r1 + beta * r0)
+    along = alpha0 * (0.5 * q + mu * u - z) + beta * (0.5 * r0 + u)
+    residual_ref[...] = r1 - alpha1 * along
 
     finish(first)
     finish(second)
@@ -382,16 +383,18 @@
     lines = pltpu.VMEM((count, 1, LANES), jnp.float32)
     hbm = pl.BlockSpec(memory_space=pltpu.HBM)
     inputs = pltpu.VMEM((blocks * band, cols // LANES, LANES), jnp.float32)
-    r0, u, z, scalars = pl.pallas_call(
+    return pl.pallas_call(
         functools.partial(solve_kernel, ny, nx, slots),
-        out_shape=(shape, shape, shape, jax.ShapeDtypeStruct((1, LANES), jnp.float32)),
+        out_shape=(shape, shape),
         in_specs=[vmem] * 2 + [hbm] * 6,
-        out_specs=(vmem,) * 4,
+        out_specs=(vmem,) * 2,
         scratch_shapes=[
             inputs,
             inputs,
             pltpu.VMEM((rows, cols), jnp.float32),
             *[pltpu.VMEM(matrix.shape, matrix.dtype) for matrix in matrices],
+            pltpu.VMEM((rows, cols), jnp.float32),
+            pltpu.VMEM((rows, cols), jnp.float32),
             pltpu.VMEM((rows, cols), jnp.float32),
             pltpu.SemaphoreType.DMA((6,)),
             chunks,
@@ -412,7 +415,7 @@
             pltpu.SemaphoreType.DMA((1,)),
         ],
         compiler_params=pltpu.CompilerParams(
-            collective_id=0, has_side_effects=True, vmem_limit_bytes=48 * 2**20
+            collective_id=0, has_side_effects=True, vmem_limit_bytes=LIMIT
         ),
     )(
         block_tile.reshape(1, blocks),
@@ -422,11 +425,6 @@
         prior_weight,
         *matrices,
     )
-    alpha0, alpha1, beta, mu = [scalars[0, index] for index in range(4)]
-    q = mu * r0 - u
-    r1 = alpha0 * q
-    along = alpha0 * (0.5 * q + mu * u - z) + beta * (0.5 * r0 + u)
-    return alpha0 * r0 + alpha1 * (r1 + beta * r0), r1 - alpha1 * along
 
 
 def solution(mesh):

time: 80.1 us -> 72.7 us (0.908)
  local copies, waits for them, and re-layouts: 7.23 us -> 2.74 us
  other arithmetic: 3.74 us -> 0 us
  Pallas kernels: 68.1 us -> 69.2 us
    unnamed x16 -> x4, local copies, waits for them, and re-layouts: 6.58 us -> 2.74 us
    sub x1 -> x0, other arithmetic: 3.74 us -> none  [shards(): return (alpha0 * r0 + alpha1 * (r1 + beta * r0), r1 - alpha1 * along)]
    pallas_call x1, Pallas kernels: 68.1 us -> 69.2 us  [shards(): pl.pallas_call(functools.partial(solve_kernel, ny, nx, slots), out_shape=...]
where the time goes in v4:
time: 72.7 us; the launch traced here: 72.6 us
  Pallas kernels  69.2 us (95%)
  local copies, waits for them, and re-layouts  2.74 us (4%)
    pallas_call x1, Pallas kernels, shards(): pl.pallas_call(functools.partial(solve_kernel, ny, nx, slots), out_shape=...  69.2 us
    unnamed x4, local copies, waits for them, and re-layouts  2.74 us

profile of v4, /device:TPU:0, one launch (start us, length us, event | category | flops | bytes accessed | tf_op | source)
XLA Modules:
  0.0 72.6 jit_solution(10135242863090231602)
XLA Ops:
  0.6 69.2 %shard_map.86 = (f32[128,1024]{1,0:T(8,128)}, f32[128,1024]{1,0:T(8,128)}) custom-call(s32[1,128]{1,0:T(1,128)} %bitcast.6, s32[1,128]{1,0:T(1,128)} %bitcast.7, f32[128,8,128]{2,1,0:T(8,128)} %bitcast.4, f32[128,8,128]{2,1,0:T(8,128)} %bitcast.5, f32[128,1024]{1,0:T(8,128)} %prior_hbm.1, bf16[256,192]{1,0:T(8,128)(2,1)} %constant.10.row_hbm, ...), custom_call_target="tpu_custom_call" | custom-call | tf_op jit(solution)/shard_map/pallas_call | solution.py:386
  69.8 0.0 copy-start
  69.8 1.9 %copy.11 = f32[128,1024]{1,0:T(8,128)} copy(f32[128,1024]{1,0:T(8,128)} %get-tuple-element.4) | data formatting | bytes 1048576
  71.8 0.0 copy-done
  71.8 0.8 %copy.12 = f32[128,1024]{1,0:T(8,128)} copy(f32[128,1024]{1,0:T(8,128)S(1)} %copy-done) | data formatting | bytes 1048576
Async XLA Ops:
  69.8 2.0 %copy-start = (f32[128,1024]{1,0:T(8,128)S(1)}, f32[128,1024]{1,0:T(8,128)}, u32[]{:S(2)}) copy-start(f32[128,1024]{1,0:T(8,128)} %get-tuple-element.5) | copy-start | bytes 1572868

commit v5 on v4

--- a/solution.py
+++ b/solution.py
@@ -10,7 +10,7 @@
 
 HALF = 32
 LANES = 128
-PIECES = 4
+PIECES = 8
 LIMIT = 60 * 1024 * 1024
 MESH = pl.DeviceIdType.MESH
 

time: 72.7 us -> 73.3 us (level)
  no operation moved by 1% of the time
where the time goes in v5:
time: 73.3 us; the launch traced here: 73.2 us
  Pallas kernels  69.8 us (95%)
  local copies, waits for them, and re-layouts  2.74 us (4%)
    pallas_call x1, Pallas kernels, shards(): pl.pallas_call(functools.partial(solve_kernel, ny, nx, slots), out_shape=...  69.8 us
    unnamed x4, local copies, waits for them, and re-layouts  2.74 us

profile of v5, /device:TPU:0, one launch (start us, length us, event | category | flops | bytes accessed | tf_op | source)
XLA Modules:
  0.0 73.2 jit_solution(14950469705436961862)
XLA Ops:
  0.6 69.8 %shard_map.86 = (f32[128,1024]{1,0:T(8,128)}, f32[128,1024]{1,0:T(8,128)}) custom-call(s32[1,128]{1,0:T(1,128)} %bitcast.6, s32[1,128]{1,0:T(1,128)} %bitcast.7, f32[128,8,128]{2,1,0:T(8,128)} %bitcast.4, f32[128,8,128]{2,1,0:T(8,128)} %bitcast.5, f32[128,1024]{1,0:T(8,128)} %prior_hbm.1, bf16[256,192]{1,0:T(8,128)(2,1)} %constant.10.row_hbm, ...), custom_call_target="tpu_custom_call" | custom-call | tf_op jit(solution)/shard_map/pallas_call | solution.py:386
  70.4 0.0 copy-start
  70.4 1.9 %copy.11 = f32[128,1024]{1,0:T(8,128)} copy(f32[128,1024]{1,0:T(8,128)} %get-tuple-element.4) | data formatting | bytes 1048576
  72.4 0.0 copy-done
  72.4 0.8 %copy.12 = f32[128,1024]{1,0:T(8,128)} copy(f32[128,1024]{1,0:T(8,128)S(1)} %copy-done) | data formatting | bytes 1048576
Async XLA Ops:
  70.4 2.0 %copy-start = (f32[128,1024]{1,0:T(8,128)S(1)}, f32[128,1024]{1,0:T(8,128)}, u32[]{:S(2)}) copy-start(f32[128,1024]{1,0:T(8,128)} %get-tuple-element.5) | copy-start | bytes 1572868
